TPU v7x, 32 devices: a whole 2x2x4 slice. The times are simulated.
32 devices in a mesh: grp: 8 (over y, x, core), top: 4 (over z).
Axes of the slice: x: 2, y: 2, z: 4, core: 2. Of those that a mesh axis runs over, the one named last changes fastest.
Arguments:
- basis_grad: float32 [8, 4, 512, 384], P('grp', 'top'), may hold values from -6 to 6
- leaf_q: float32 [8, 4, 512, 384], P('grp', 'top'), may hold values from -0.25 to 0.25
- leaf_rinv: float32 [8, 4, 384, 384], P('grp', 'top'), may hold values from -5 to 4, as said below
- merge_q1: float32 [8, 4, 384, 384], P('grp', 'top'), may hold values from -0.3125 to 0.3125
- merge_q2: float32 [4, 384, 384], P('top', 'grp'), may hold values from -0.15625 to 0.15625
Outputs:
- data_grad: float32 [8, 4, 512, 384], P('grp', 'top')
Inputs may be any that keep to these rules, and one draw needn't show every extreme that they name: Each leaf_rinv[i,g] is upper triangular with a diagonal between 1 and 4.
All inputs are finite; a program needn't handle non-finite values.
Results may differ from a plain program's by a relative error of at most 0.00023.
Values sent between devices are 32-bit elements; how exact they have to be, the bound alone decides.
A program may use at most 64 MiB of HBM per device.

v0:
```python
import jax
import jax.numpy as jnp
from jax import lax
from jax.sharding import PartitionSpec as P

highest = lax.Precision.HIGHEST


def product(former, latter, former_dim, latter_dim):
    return lax.dot_general(
        former,
        latter,
        (((former_dim,), (latter_dim,)), ((), ())),
        precision=highest,
        preferred_element_type=jnp.float32,
    )


def symmetrize(matrix):
    return jnp.tril(matrix) + jnp.tril(matrix, -1).T


def per_device(basis_grad, leaf_q, leaf_rinv, merge_q1, merge_q2):
    cotangent = basis_grad[0, 0]
    leaf_basis = leaf_q[0, 0]
    inverse = leaf_rinv[0, 0]
    first_block = merge_q1[0, 0]
    second_factor = lax.all_gather(merge_q2[0], "grp", axis=0, tiled=True)
    projected = product(leaf_basis, cotangent, 0, 0)
    combined = product(first_block, second_factor, 1, 0)
    leaf_cotan = product(cotangent, combined, 1, 1)
    first_cotan = product(projected, second_factor, 1, 1)
    second_term = product(first_block, projected, 0, 0)
    gram_term = product(first_cotan, first_block, 0, 0)
    second_cotan, group_gram = lax.psum((second_term, gram_term), "grp")
    top_adjoint = lax.psum(-product(second_cotan, second_factor, 0, 0), "top")
    top_sym = symmetrize(top_adjoint)
    group_back = product(second_cotan + product(second_factor, top_sym, 1, 0), second_factor, 1, 1)
    group_adjoint = group_back.T - group_gram
    group_sym = symmetrize(group_adjoint)
    leaf_back = product(first_cotan + product(first_block, group_sym, 1, 0), first_block, 1, 1)
    leaf_adjoint = leaf_back.T - product(leaf_cotan, leaf_basis, 0, 0)
    leaf_sym = symmetrize(leaf_adjoint)
    inner = leaf_cotan + product(leaf_basis, leaf_sym, 1, 0)
    result = product(inner, inverse, 1, 1)
    return result[None, None]


def solution(mesh):
    placed = (
        P("grp", "top", None, None),
        P("grp", "top", None, None),
        P("grp", "top", None, None),
        P("grp", "top", None, None),
        P("top", "grp", None),
    )
    return jax.shard_map(
        per_device,
        mesh=mesh,
        in_specs=placed,
        out_specs=P("grp", "top", None, None),
        check_vma=False,
    )
```

profile of v0, /device:TPU:0, one launch (start us, length us, event | category | flops | bytes accessed | tf_op | source)
XLA Modules:
  0.0 153.7 jit_solution(6126031068514458693)
XLA Ops:
  6.5 0.0 copy-start
  6.5 0.0 all-reduce.6.cloned.1.call-start
  6.5 11.9 %all-gather = f32[1,384,384]{2,1,0:T(8,128)S(1)} all-gather(f32[1,48,384]{2,1,0:T(8,128)} %param.9), channel_id=2, replica_groups=mesh['grp'=8,'top'=4] {'grp'}, dimensions={1}, use_global_device_ids=true | all-gather | bytes 663552 | tf_op jit(solution)/shard_map/all_gather | solution.py:28
  18.4 0.0 copy-done
  18.4 2.6 %fusion.6 = f32[384,384]{1,0:T(8,128)S(1)} fusion(f32[1,1,512,384]{3,2,1,0:T(8,128)S(1)} %copy-done, f32[1,1,512,384]{3,2,1,0:T(8,128)} %param.5), kind=kOutput, calls=%fused_computation.13 | convolution fusion | flops 905969664 | bytes 2162688 | tf_op jit(solution)/shard_map/dot_general | solution.py:10
  21.0 0.0 copy-start.1
  21.0 1.3 fusion.20
  22.3 0.0 copy-done.1
  22.3 2.1 %convolution_bitcast_fusion.4 = f32[384,384]{0,1:T(8,128)} fusion(f32[384,384]{1,0:T(8,128)S(1)} %fusion.6, f32[1,1,384,384]{3,2,1,0:T(8,128)S(1)} %copy-done.1), kind=kOutput, calls=%fused_computation.9 | convolution fusion | flops 679477248 | bytes 1769472 | tf_op jit(solution)/shard_map/dot_general | solution.py:10
  24.4 2.2 %fusion.27 = f32[384,384]{1,0:T(8,128)} fusion(f32[384,384]{1,0:T(8,128)S(1)} %fusion.20, f32[1,1,384,384]{3,2,1,0:T(8,128)S(1)} %copy-done.1), kind=kOutput, calls=%fused_computation.36 | convolution fusion | flops 679477248 | bytes 1769472 | tf_op jit(solution)/shard_map/dot_general | solution.py:10
  26.6 0.0 all-reduce.6.cloned.1.call-update
  26.6 0.2 all-reduce.4.cloned.1.call-start
  26.8 2.1 %fusion.22 = f32[384,384]{1,0:T(8,128)} fusion(f32[1,384,384]{2,1,0:T(8,128)S(1)} %all-gather, f32[1,1,384,384]{3,2,1,0:T(8,128)S(1)} %copy-done.1), kind=kOutput, calls=%fused_computation.31 | convolution fusion | flops 679477248 | bytes 1769472 | tf_op jit(solution)/shard_map/dot_general | solution.py:10
  28.9 55.3 %all-reduce.6.cloned.1.call-done = (f32[384,384]{1,0:T(8,128)}, f32[384,384]{0,1:T(8,128)}) async-done(((f32[384,384]{1,0:T(8,128)}, f32[384,384]{0,1:T(8,128)}), (f32[384,384]{1,0:T(8,128)}, f32[384,384]{0,1:T(8,128)})) %all-reduce.6.cloned.1.call-update) | async-done | bytes 1179664 | tf_op jit(solution)/shard_map/psum | solution.py:35
  84.2 3.1 %convolution_negate_fusion = f32[384,384]{1,0:T(8,128)} fusion(f32[384,384]{0,1:T(8,128)} %get-tuple-element.6, f32[1,384,384]{2,1,0:T(8,128)S(1)} %all-gather), kind=kOutput, calls=%fused_computation.8 | convolution fusion | flops 679624704 | bytes 1769472 | tf_op jit(solution)/shard_map/dot_general | solution.py:10
  87.4 0.0 all-reduce.4.cloned.1.call-update
  87.4 2.7 %fusion.9 = f32[384,512]{1,0:T(8,128)S(1)} fusion(f32[384,384]{1,0:T(8,128)} %fusion.22, f32[1,1,512,384]{3,2,1,0:T(8,128)} %param.5), kind=kOutput, calls=%fused_computation.16 | convolution fusion | flops 905969664 | bytes 2162688 | tf_op jit(solution)/shard_map/dot_general | solution.py:10
  90.2 2.2 %fusion.4 = f32[384,384]{1,0:T(8,128)} fusion(f32[384,512]{1,0:T(8,128)S(1)} %fusion.9, f32[1,1,512,384]{3,2,1,0:T(8,128)S(1)} %copy-done), kind=kOutput, calls=%fused_computation.11 | convolution fusion | flops 905969664 | bytes 2162688 | tf_op jit(solution)/shard_map/dot_general | solution.py:10
  92.4 2.1 %copy.11 = f32[384,384]{0,1:T(8,128)} copy(f32[384,384]{1,0:T(8,128)} %fusion.4) | data formatting | bytes 1179648 | tf_op jit(solution)/shard_map/dot_general | solution.py:10
  94.5 31.5 %all-reduce.4.cloned.1.call-done = f32[384,384]{1,0:T(8,128)} async-done(((f32[384,384]{1,0:T(8,128)}), f32[384,384]{1,0:T(8,128)}) %all-reduce.4.cloned.1.call-update) | async-done | bytes 589840 | tf_op jit(solution)/shard_map/psum | solution.py:36
  126.0 2.1 %copy.6 = f32[384,384]{0,1:T(8,128)} copy(f32[384,384]{1,0:T(8,128)} %all-reduce.4.cloned.1.call-done) | data formatting | bytes 1179648 | tf_op jit(solution)/shard_map/psum | solution.py:36
  128.1 2.8 %fusion.2 = f32[384,384]{0,1:T(8,128)S(1)} fusion(f32[384,384]{0,1:T(8,128)} %get-tuple-element.6, f32[1,384,384]{2,1,0:T(8,128)S(1)} %all-gather, f32[384,384]{1,0:T(8,128)} %all-reduce.4.cloned.1.call-done, f32[384,384]{0,1:T(8,128)} %copy.6, s32[384]{0:T(512)S(1)} %iota_add_fusion), kind=kOutput, calls=%fused_computation.7 | convolution fusion | flops 680361984 | bytes 2950656 | tf_op jit(solution)/shard_map/dot_general | solution.py:10
  131.0 2.1 %fusion.1 = f32[384,384]{1,0:T(8,128)} fusion(f32[384,384]{1,0:T(8,128)S(1)} %copy-done.6, f32[384,384]{0,1:T(8,128)S(1)} %fusion.2, f32[1,384,384]{2,1,0:T(8,128)S(1)} %all-gather), kind=kOutput, calls=%fused_computation.5 | convolution fusion | flops 679624704 | bytes 2359296 | tf_op jit(solution)/shard_map/dot_general | solution.py:10
  133.1 2.2 %copy.9 = f32[384,384]{0,1:T(8,128)} copy(f32[384,384]{1,0:T(8,128)} %fusion.1) | data formatting | bytes 1179648 | tf_op jit(solution)/shard_map/sub | solution.py:39
  135.3 2.5 %fusion = f32[384,384]{1,0:T(8,128)S(1)} fusion(f32[384,384]{1,0:T(8,128)S(1)} %fusion.20, f32[1,1,384,384]{3,2,1,0:T(8,128)S(1)} %copy-done.1, f32[384,384]{1,0:T(8,128)S(1)} %copy-done.2, f32[384,384]{0,1:T(8,128)} %copy.9, s32[384]{0:T(512)S(1)} %iota_add_fusion), kind=kOutput, calls=%fused_computation.3 | convolution fusion | flops 680361984 | bytes 2950656 | tf_op jit(solution)/shard_map/dot_general | solution.py:10
  137.7 1.3 fusion.24
  139.0 1.1 copy.12
  140.1 0.0 copy-done.3
  140.1 0.4 copy-done.4
  140.5 2.9 %convolution_add_fusion = f32[384,512]{1,0:T(8,128)S(1)} fusion(f32[384,512]{1,0:T(8,128)S(1)} %fusion.9, f32[1,1,512,384]{3,2,1,0:T(8,128)S(1)} %copy-done, f32[384,384]{0,1:T(8,128)} %copy.12, f32[384,384]{1,0:T(8,128)S(1)} %copy-done.3, f32[384,384]{0,1:T(8,128)S(1)} %copy-done.4, f32[384,384]{1,0:T(8,128)S(1)} %fusion.24, s32[384]{0:T(512)S(1)} %iota_add_fusion), kind=kOutput, calls=%fused_computation.1 | convolution fusion | flops 907198464 | bytes 4720128 | tf_op jit(solution)/shard_map/dot_general | solution.py:10
  143.4 0.0 copy-done.5
  143.4 3.5 %convolution_bitcast_fusion = f32[1,1,512,384]{3,2,1,0:T(8,128)} fusion(f32[384,512]{1,0:T(8,128)S(1)} %convolution_add_fusion, f32[1,1,384,384]{3,2,1,0:T(8,128)S(1)} %copy-done.5), kind=kOutput, calls=%fused_computation | convolution fusion | flops 905969664 | bytes 2162688 | tf_op jit(solution)/shard_map/dot_general | solution.py:10
  (8 shorter events, 0.0 us)
Async XLA Ops:
  6.5 11.9 %copy-start = (f32[1,1,512,384]{3,2,1,0:T(8,128)S(1)}, f32[1,1,512,384]{3,2,1,0:T(8,128)}, u32[]{:S(2)}) copy-start(f32[1,1,512,384]{3,2,1,0:T(8,128)} %param.6) | copy-start | bytes 2359300
  6.5 77.7 %all-reduce.6.cloned.1.call-start = ((), (), s32[]{:S(2)}) async-start(), calls=%async_computation.1 | async-start | bytes 2359296 | tf_op jit(solution)/shard_map/psum | solution.py:35
  21.0 1.3 copy-start.1
  26.6 99.4 %all-reduce.4.cloned.1.call-start = ((), (), s32[]{:S(2)}) async-start(), calls=%async_computation | async-start | bytes 1179648 | tf_op jit(solution)/shard_map/psum | solution.py:36
  128.1 2.9 %copy-start.6 = (f32[384,384]{1,0:T(8,128)S(1)}, f32[384,384]{1,0:T(8,128)}, u32[]{:S(2)}) copy-start(f32[384,384]{1,0:T(8,128)} %get-tuple-element.5) | copy-start | bytes 1769476
  133.1 2.2 %copy-start.2 = (f32[384,384]{1,0:T(8,128)S(1)}, f32[384,384]{1,0:T(8,128)}, u32[]{:S(2)}) copy-start(f32[384,384]{1,0:T(8,128)} %fusion.1) | copy-start | bytes 1769476
  139.0 1.1 copy-start.3
  139.0 1.4 copy-start.4
  140.5 2.9 %copy-start.5 = (f32[1,1,384,384]{3,2,1,0:T(8,128)S(1)}, f32[1,1,384,384]{3,2,1,0:T(8,128)}, u32[]{:S(2)}) copy-start(f32[1,1,384,384]{3,2,1,0:T(8,128)} %param.7) | copy-start | bytes 1769476
Sparse Core Ops, SparseCore 0:
  26.7 57.4 all-reduce.5
  87.5 38.4 all-reduce.3
where the time goes:
time: 154 us
  waiting for transfers between devices  86.8 us (56%)
  matrix products  33.4 us (22%)
  between operations  13.5 us (9%)
  blocking collectives  11.9 us (8%)
  local copies, waits for them, and re-layouts  7.88 us (5%)
    psum x1, waiting for transfers between devices, per_device(): second_cotan, group_gram = lax.psum((second_term, gram_term), 'grp')  55.3 us
    dot_general x14, matrix products, product(): lax.dot_general(former, latter, (((former_dim,), (latter_dim,)), ((), ())...  33.4 us
    psum x1, waiting for transfers between devices, per_device(): top_adjoint = lax.psum(-product(second_cotan, second_factor, 0, 0), 'top')  31.5 us
    all_gather x1, blocking collectives, per_device(): second_factor = lax.all_gather(merge_q2[0], 'grp', axis=0, tiled=True)  11.9 us
    dot_general x2, local copies, waits for them, and re-layouts, product(): lax.dot_general(former, latter, (((former_dim,), (latter_dim,)), ((), ())...  3.17 us
  transfers between devices with their start and end apart: 2, of which 2 were waited for; matrix products, arithmetic and copies ran while one was open for 6% of the time, Pallas kernels for 0%

commit v1 on v0

--- a/solution.py
+++ b/solution.py
@@ -25,7 +25,18 @@
     leaf_basis = leaf_q[0, 0]
     inverse = leaf_rinv[0, 0]
     first_block = merge_q1[0, 0]
-    second_factor = lax.all_gather(merge_q2[0], "grp", axis=0, tiled=True)
+    size, here, extent = (lax.axis_size("grp"), lax.axis_index("grp"), merge_q2[0].shape[0])
+    right = [(i, (i + 1) % size) for i in range(size)]
+    result_2 = jnp.zeros(
+        (*merge_q2[0].shape[:0], size * extent, *merge_q2[0].shape[0 + 1 :]), merge_q2[0].dtype
+    )
+    held = merge_q2[0]
+    for turn in range(size):
+        source = (here - turn) % size
+        result_2 = lax.dynamic_update_slice_in_dim(result_2, held, source * extent, axis=0)
+        if turn < size - 1:
+            held = lax.ppermute(held, "grp", right)
+    second_factor = result_2
     projected = product(leaf_basis, cotangent, 0, 0)
     combined = product(first_block, second_factor, 1, 0)
     leaf_cotan = product(cotangent, combined, 1, 1)

time: 154 us -> 193 us (1.25)
  waiting for transfers between devices: 86.8 us -> 124 us
  local copies, waits for them, and re-layouts: 7.88 us -> 22.7 us
  blocking collectives: 11.9 us -> 0 us
    ppermute x0 -> x7, waiting for transfers between devices: none -> 33.6 us  [per_device(): held = lax.ppermute(held, 'grp', right)]
    dynamic_update_slice x0 -> x8, local copies, waits for them, and re-layouts: none -> 14 us  [per_device(): lax.dynamic_update_slice_in_dim(result_2, held, source * extent, axis=0)]
    all_gather x1 -> x0, blocking collectives: 11.9 us -> none  [per_device(): second_factor = lax.all_gather(merge_q2[0], 'grp', axis=0, tiled=True)]
    psum x1, waiting for transfers between devices: 55.3 us -> 59.4 us  [per_device(): second_cotan, group_gram = lax.psum((second_term, gram_term), 'grp')]
  transfers between devices with their start and end apart: 2 -> 9, of which waited for: 2 -> 8; matrix products, arithmetic and copies ran while one was open for 6% -> 13% of each run, Pallas kernels for 0% -> 0%
where the time goes in v1:
time: 193 us
  waiting for transfers between devices  124 us (64%)
  matrix products  31.8 us (16%)
  local copies, waits for them, and re-layouts  22.7 us (12%)
  between operations  13.9 us (7%)
    psum x1, waiting for transfers between devices, per_device(): second_cotan, group_gram = lax.psum((second_term, gram_term), 'grp')  59.4 us
    ppermute x7, waiting for transfers between devices, per_device(): held = lax.ppermute(held, 'grp', right)  33.6 us
    dot_general x14, matrix products, product(): lax.dot_general(former, latter, (((former_dim,), (latter_dim,)), ((), ())...  31.8 us
    psum x1, waiting for transfers between devices, per_device(): top_adjoint = lax.psum(-product(second_cotan, second_factor, 0, 0), 'top')  30.8 us
    dynamic_update_slice x8, local copies, waits for them, and re-layouts, per_device(): lax.dynamic_update_slice_in_dim(result_2, held, source * extent, axis=0)  14 us
  transfers between devices with their start and end apart: 9, of which 8 were waited for; matrix products, arithmetic and copies ran while one was open for 13% of the time, Pallas kernels for 0%

profile of v1, /device:TPU:0, one launch (start us, length us, event | category | flops | bytes accessed | tf_op | source)
XLA Modules:
  0.0 193.0 jit_solution(7027496299067142320)
XLA Ops:
  8.1 6.2 %collective-permute-done = f32[48,384]{0,1:T(8,128)S(1)} collective-permute-done((f32[48,384]{0,1:T(8,128)S(1)}, f32[48,384]{0,1:T(8,128)S(1)}, u32[]{:S(2)}, u32[]{:S(2)}) %collective-permute-start) | collective-permute-done | bytes 73760 | tf_op jit(solution)/shard_map/ppermute | solution.py:38
  14.4 6.0 %collective-permute-done.1 = f32[48,384]{0,1:T(8,128)S(1)} collective-permute-done((f32[48,384]{0,1:T(8,128)S(1)}, f32[48,384]{0,1:T(8,128)S(1)}, u32[]{:S(2)}, u32[]{:S(2)}) %collective-permute-start.1) | collective-permute-done | bytes 73760 | tf_op jit(solution)/shard_map/ppermute | solution.py:38
  20.4 6.0 %collective-permute-done.2 = f32[48,384]{0,1:T(8,128)S(1)} collective-permute-done((f32[48,384]{0,1:T(8,128)S(1)}, f32[48,384]{0,1:T(8,128)S(1)}, u32[]{:S(2)}, u32[]{:S(2)}) %collective-permute-start.2) | collective-permute-done | bytes 73760 | tf_op jit(solution)/shard_map/ppermute | solution.py:38
  26.4 6.0 %collective-permute-done.3 = f32[48,384]{0,1:T(8,128)S(1)} collective-permute-done((f32[48,384]{0,1:T(8,128)S(1)}, f32[48,384]{0,1:T(8,128)S(1)}, u32[]{:S(2)}, u32[]{:S(2)}) %collective-permute-start.3) | collective-permute-done | bytes 73760 | tf_op jit(solution)/shard_map/ppermute | solution.py:38
  32.4 6.0 %collective-permute-done.4 = f32[48,384]{0,1:T(8,128)S(1)} collective-permute-done((f32[48,384]{0,1:T(8,128)S(1)}, f32[48,384]{0,1:T(8,128)S(1)}, u32[]{:S(2)}, u32[]{:S(2)}) %collective-permute-start.4) | collective-permute-done | bytes 73760 | tf_op jit(solution)/shard_map/ppermute | solution.py:38
  38.4 2.6 %fusion.4 = f32[384,384]{1,0:T(8,128)S(1)} fusion(f32[1,1,512,384]{3,2,1,0:T(8,128)S(1)} %copy-done, f32[1,1,512,384]{3,2,1,0:T(8,128)} %param.5), kind=kOutput, calls=%fused_computation.11 | convolution fusion | flops 905969664 | bytes 2162688 | tf_op jit(solution)/shard_map/dot_general | solution.py:10
  41.0 3.4 %collective-permute-done.5 = f32[48,384]{0,1:T(8,128)} collective-permute-done((f32[48,384]{0,1:T(8,128)S(1)}, f32[48,384]{0,1:T(8,128)}, u32[]{:S(2)}, u32[]{:S(2)}) %collective-permute-start.5) | collective-permute-done | bytes 73760 | tf_op jit(solution)/shard_map/ppermute | solution.py:38
  44.5 2.1 %convolution_bitcast_fusion.2 = f32[384,384]{0,1:T(8,128)} fusion(f32[384,384]{1,0:T(8,128)S(1)} %fusion.4, f32[1,1,384,384]{3,2,1,0:T(8,128)S(1)} %copy-done.1), kind=kOutput, calls=%fused_computation.7 | convolution fusion | flops 679477248 | bytes 1769472 | tf_op jit(solution)/shard_map/dot_general | solution.py:10
  46.7 1.5 dynamic_update_slice.24
  48.2 1.2 dynamic_update_slice.25
  50.6 1.8 dynamic_update_slice.27
  52.4 1.8 dynamic_update_slice.28
  54.3 1.8 dynamic_update_slice.29
  56.1 2.3 %dynamic_update_slice.30 = f32[384,384]{0,1:T(8,128)S(1)} dynamic-update-slice(f32[384,384]{0,1:T(8,128)S(1)} %dynamic_update_slice.29, f32[48,384]{0,1:T(8,128)} %collective-permute-done.5, s32[]{:T(128)S(6)} %select_n.93, s32[]{:T(128)} %constant.75.clone.1) | dynamic-update-slice | bytes 147460 | tf_op jit(solution)/shard_map/dynamic_update_slice | solution.py:36
  58.4 2.3 %dynamic_update_slice.31 = f32[384,384]{0,1:T(8,128)S(1)} dynamic-update-slice(f32[384,384]{0,1:T(8,128)S(1)} %dynamic_update_slice.30, f32[48,384]{0,1:T(8,128)} %collective-permute-done.6, s32[]{:T(128)S(6)} %select_n.95, s32[]{:T(128)} %constant.75.clone.1) | dynamic-update-slice | bytes 147460 | tf_op jit(solution)/shard_map/dynamic_update_slice | solution.py:36
  60.8 1.3 fusion.38
  62.1 2.1 %fusion.18 = f32[384,384]{1,0:T(8,128)} fusion(f32[384,384]{1,0:T(8,128)S(1)} %fusion.38, f32[1,1,384,384]{3,2,1,0:T(8,128)S(1)} %copy-done.1), kind=kOutput, calls=%fused_computation.27 | convolution fusion | flops 679477248 | bytes 1769472 | tf_op jit(solution)/shard_map/dot_general | solution.py:10
  64.5 59.4 %all-reduce.6.cloned.1.call-done = (f32[384,384]{1,0:T(8,128)}, f32[384,384]{0,1:T(8,128)}) async-done(((f32[384,384]{1,0:T(8,128)}, f32[384,384]{0,1:T(8,128)}), (f32[384,384]{1,0:T(8,128)}, f32[384,384]{0,1:T(8,128)})) %all-reduce.6.cloned.1.call-update) | async-done | bytes 1179664 | tf_op jit(solution)/shard_map/psum | solution.py:46
  123.8 3.1 %convolution_negate_fusion = f32[384,384]{1,0:T(8,128)} fusion(f32[384,384]{0,1:T(8,128)} %get-tuple-element.6, f32[384,384]{0,1:T(8,128)S(1)} %dynamic_update_slice.31), kind=kOutput, calls=%fused_computation.6 | convolution fusion | flops 679624704 | bytes 1769472 | tf_op jit(solution)/shard_map/dot_general | solution.py:10
  127.0 1.3 fusion.21
  128.3 2.1 %fusion.7 = f32[384,512]{1,0:T(8,128)S(1)} fusion(f32[384,384]{1,0:T(8,128)S(1)} %fusion.21, f32[1,1,512,384]{3,2,1,0:T(8,128)S(1)} %copy-done.4), kind=kOutput, calls=%fused_computation.14 | convolution fusion | flops 905969664 | bytes 2162688 | tf_op jit(solution)/shard_map/dot_general | solution.py:10
  130.4 2.2 %fusion.2 = f32[384,384]{1,0:T(8,128)} fusion(f32[384,512]{1,0:T(8,128)S(1)} %fusion.7, f32[1,1,512,384]{3,2,1,0:T(8,128)S(1)} %copy-done), kind=kOutput, calls=%fused_computation.9 | convolution fusion | flops 905969664 | bytes 2162688 | tf_op jit(solution)/shard_map/dot_general | solution.py:10
  132.6 2.1 %copy.11 = f32[384,384]{0,1:T(8,128)} copy(f32[384,384]{1,0:T(8,128)} %fusion.2) | data formatting | bytes 1179648 | tf_op jit(solution)/shard_map/dot_general | solution.py:10
  134.7 30.8 %all-reduce.4.cloned.1.call-done = f32[384,384]{1,0:T(8,128)} async-done(((f32[384,384]{1,0:T(8,128)}), f32[384,384]{1,0:T(8,128)}) %all-reduce.4.cloned.1.call-update) | async-done | bytes 589840 | tf_op jit(solution)/shard_map/psum | solution.py:47
  165.6 2.1 %copy.7 = f32[384,384]{0,1:T(8,128)} copy(f32[384,384]{1,0:T(8,128)} %all-reduce.4.cloned.1.call-done) | data formatting | bytes 1179648 | tf_op jit(solution)/shard_map/psum | solution.py:47
  167.7 2.8 %convolution_add_fusion.1 = f32[384,384]{0,1:T(8,128)S(1)} fusion(f32[384,384]{0,1:T(8,128)} %get-tuple-element.6, f32[384,384]{0,1:T(8,128)S(1)} %dynamic_update_slice.31, f32[384,384]{1,0:T(8,128)} %all-reduce.4.cloned.1.call-done, f32[384,384]{0,1:T(8,128)} %copy.7, s32[384]{0:T(512)S(1)} %iota_add_fusion), kind=kOutput, calls=%fused_computation.3 | convolution fusion | flops 680361984 | bytes 2950656 | tf_op jit(solution)/shard_map/dot_general | solution.py:10
  170.5 2.1 %convolution_subtract_fusion = f32[384,384]{1,0:T(8,128)} fusion(f32[384,384]{1,0:T(8,128)S(1)} %copy-done.7, f32[384,384]{0,1:T(8,128)S(1)} %dynamic_update_slice.31, f32[384,384]{0,1:T(8,128)S(1)} %convolution_add_fusion.1), kind=kOutput, calls=%fused_computation.2 | convolution fusion | flops 679624704 | bytes 2359296 | tf_op jit(solution)/shard_map/dot_general | solution.py:10
  172.6 2.2 %copy.9 = f32[384,384]{0,1:T(8,128)} copy(f32[384,384]{1,0:T(8,128)} %convolution_subtract_fusion) | data formatting | bytes 1179648 | tf_op jit(solution)/shard_map/sub | solution.py:50
  174.8 2.5 %fusion = f32[384,384]{1,0:T(8,128)S(1)} fusion(f32[384,384]{1,0:T(8,128)S(1)} %fusion.38, f32[1,1,384,384]{3,2,1,0:T(8,128)S(1)} %copy-done.1, f32[384,384]{1,0:T(8,128)S(1)} %copy-done.2, f32[384,384]{0,1:T(8,128)} %copy.9, s32[384]{0:T(512)S(1)} %iota_add_fusion), kind=kOutput, calls=%fused_computation.5 | convolution fusion | flops 680361984 | bytes 2950656 | tf_op jit(solution)/shard_map/dot_general | solution.py:10
  177.3 1.3 fusion.15
  179.9 2.7 %convolution_add_fusion = f32[384,512]{1,0:T(8,128)S(1)} fusion(f32[384,512]{1,0:T(8,128)S(1)} %fusion.7, f32[1,1,512,384]{3,2,1,0:T(8,128)S(1)} %copy-done, f32[384,384]{0,1:T(8,128)} %copy.12, f32[384,384]{1,0:T(8,128)S(1)} %copy-done.3, f32[384,384]{0,1:T(8,128)S(1)} %copy-done.5, f32[384,384]{1,0:T(8,128)S(1)} %fusion.15, s32[384]{0:T(512)S(1)} %iota_add_fusion), kind=kOutput, calls=%fused_computation.1 | convolution fusion | flops 907198464 | bytes 4720128 | tf_op jit(solution)/shard_map/dot_general | solution.py:10
  182.6 3.5 %convolution_bitcast_fusion = f32[1,1,512,384]{3,2,1,0:T(8,128)} fusion(f32[384,512]{1,0:T(8,128)S(1)} %convolution_add_fusion, f32[1,1,384,384]{3,2,1,0:T(8,128)S(1)} %copy-done.6), kind=kOutput, calls=%fused_computation | convolution fusion | flops 905969664 | bytes 2162688 | tf_op jit(solution)/shard_map/dot_general | solution.py:10
  (37 shorter events, 4.2 us)
Async XLA Ops:
  6.5 31.8 %copy-start = (f32[1,1,512,384]{3,2,1,0:T(8,128)S(1)}, f32[1,1,512,384]{3,2,1,0:T(8,128)}, u32[]{:S(2)}) copy-start(f32[1,1,512,384]{3,2,1,0:T(8,128)} %param.6) | copy-start | bytes 2359300
  6.5 117.3 %all-reduce.6.cloned.1.call-start = ((), (), s32[]{:S(2)}) async-start(), calls=%async_computation.1 | async-start | bytes 2359296 | tf_op jit(solution)/shard_map/psum | solution.py:46
  7.6 36.8 %copy-start.1 = (f32[1,1,384,384]{3,2,1,0:T(8,128)S(1)}, f32[1,1,384,384]{3,2,1,0:T(8,128)}, u32[]{:S(2)}) copy-start(f32[1,1,384,384]{3,2,1,0:T(8,128)} %param.8) | copy-start | bytes 1769476
  7.6 6.7 %collective-permute-start = (f32[48,384]{0,1:T(8,128)S(1)}, f32[48,384]{0,1:T(8,128)S(1)}, u32[]{:S(2)}, u32[]{:S(2)}) collective-permute-start(f32[48,384]{0,1:T(8,128)S(1)} %bitcast.69), channel_id=1, source_target_pairs={{0,4},{4,8},{8,12},{12,16},{16,20},{20,24},{24,28},{28,0},{1,5},{5... | collective-permute-start | bytes 221192 | tf_op jit(solution)/shard_map/ppermute | solution.py:38
  14.4 6.0 %collective-permute-start.1 = (f32[48,384]{0,1:T(8,128)S(1)}, f32[48,384]{0,1:T(8,128)S(1)}, u32[]{:S(2)}, u32[]{:S(2)}) collective-permute-start(f32[48,384]{0,1:T(8,128)S(1)} %collective-permute-done), channel_id=1, source_target_pairs={{0,4},{4,8},{8,12},{12,16},{16,20},{20,24},{24,28},{28,0},{1,5},{5... | collective-permute-start | bytes 221192 | tf_op jit(solution)/shard_map/ppermute | solution.py:38
  20.4 6.0 %collective-permute-start.2 = (f32[48,384]{0,1:T(8,128)S(1)}, f32[48,384]{0,1:T(8,128)S(1)}, u32[]{:S(2)}, u32[]{:S(2)}) collective-permute-start(f32[48,384]{0,1:T(8,128)S(1)} %collective-permute-done.1), channel_id=1, source_target_pairs={{0,4},{4,8},{8,12},{12,16},{16,20},{20,24},{24,28},{28,0},{1,5},{5... | collective-permute-start | bytes 221192 | tf_op jit(solution)/shard_map/ppermute | solution.py:38
  26.4 6.0 %collective-permute-start.3 = (f32[48,384]{0,1:T(8,128)S(1)}, f32[48,384]{0,1:T(8,128)S(1)}, u32[]{:S(2)}, u32[]{:S(2)}) collective-permute-start(f32[48,384]{0,1:T(8,128)S(1)} %collective-permute-done.2), channel_id=1, source_target_pairs={{0,4},{4,8},{8,12},{12,16},{16,20},{20,24},{24,28},{28,0},{1,5},{5... | collective-permute-start | bytes 221192 | tf_op jit(solution)/shard_map/ppermute | solution.py:38
  32.4 6.0 %collective-permute-start.4 = (f32[48,384]{0,1:T(8,128)S(1)}, f32[48,384]{0,1:T(8,128)S(1)}, u32[]{:S(2)}, u32[]{:S(2)}) collective-permute-start(f32[48,384]{0,1:T(8,128)S(1)} %collective-permute-done.3), channel_id=1, source_target_pairs={{0,4},{4,8},{8,12},{12,16},{16,20},{20,24},{24,28},{28,0},{1,5},{5... | collective-permute-start | bytes 221192 | tf_op jit(solution)/shard_map/ppermute | solution.py:38
  38.4 2.7 %copy-start.8 = (f32[48,384]{0,1:T(8,128)}, f32[48,384]{0,1:T(8,128)S(1)}, u32[]{:S(2)}) copy-start(f32[48,384]{0,1:T(8,128)S(1)} %collective-permute-done.4) | copy-start | bytes 221188
  38.4 6.1 %collective-permute-start.5 = (f32[48,384]{0,1:T(8,128)S(1)}, f32[48,384]{0,1:T(8,128)}, u32[]{:S(2)}, u32[]{:S(2)}) collective-permute-start(f32[48,384]{0,1:T(8,128)S(1)} %collective-permute-done.4), channel_id=1, source_target_pairs={{0,4},{4,8},{8,12},{12,16},{16,20},{20,24},{24,28},{28,0},{1,5},{5... | collective-permute-start | bytes 221192 | tf_op jit(solution)/shard_map/ppermute | solution.py:38
  44.5 14.0 %collective-permute-start.6 = (f32[48,384]{0,1:T(8,128)}, f32[48,384]{0,1:T(8,128)}, u32[]{:S(2)}, u32[]{:S(2)}) collective-permute-start(f32[48,384]{0,1:T(8,128)} %collective-permute-done.5), channel_id=1, source_target_pairs={{0,4},{4,8},{8,12},{12,16},{16,20},{20,24},{24,28},{28,0},{1,5},{5... | collective-permute-start | bytes 221192 | tf_op jit(solution)/shard_map/ppermute | solution.py:38
  52.4 1.9 copy-start.9
  64.2 101.4 %all-reduce.4.cloned.1.call-start = ((), (), s32[]{:S(2)}) async-start(), calls=%async_computation | async-start | bytes 1179648 | tf_op jit(solution)/shard_map/psum | solution.py:47
  127.0 1.3 copy-start.4
  167.7 2.8 %copy-start.7 = (f32[384,384]{1,0:T(8,128)S(1)}, f32[384,384]{1,0:T(8,128)}, u32[]{:S(2)}) copy-start(f32[384,384]{1,0:T(8,128)} %get-tuple-element.5) | copy-start | bytes 1769476
  172.6 2.2 %copy-start.2 = (f32[384,384]{1,0:T(8,128)S(1)}, f32[384,384]{1,0:T(8,128)}, u32[]{:S(2)}) copy-start(f32[384,384]{1,0:T(8,128)} %convolution_subtract_fusion) | copy-start | bytes 1769476
  178.6 1.3 copy-start.3
  178.8 1.1 copy-start.5
  179.9 2.7 %copy-start.6 = (f32[1,1,384,384]{3,2,1,0:T(8,128)S(1)}, f32[1,1,384,384]{3,2,1,0:T(8,128)}, u32[]{:S(2)}) copy-start(f32[1,1,384,384]{3,2,1,0:T(8,128)} %param.7) | copy-start | bytes 1769476
Sparse Core Ops, SparseCore 0:
  64.3 59.4 all-reduce.5
  127.1 38.4 all-reduce.3
